TPU v7x, 32 devices: a whole 2x2x4 slice. The times are simulated.
32 devices in a mesh: parts: 2 (over y), pol: 4 (over z), scen: 2 (over x), fund: 2 (over core).
Axes of the slice: x: 2, y: 2, z: 4, core: 2. Of those that a mesh axis runs over, the one named last changes fastest.
Arguments:
- count_init: float32 [32768], P(('pol', 'fund')), may hold values from 0.5 to 2
- value_init: float32 [32768], P(('pol', 'fund')), may hold values from 0.5 to 4
- durations: int32 [32768], P(('pol', 'fund')), may hold values from 0 to 119
- products: int32 [32768], P(('pol', 'fund')), may hold values from 0 to 7
- policy_fund: int32 [32768], P(('pol', 'fund')), may hold values from 0 to 119, as said below
- lapse_base: float32 [8], replicated, may hold values from 0.05 to 0.1
- lapse_sens: float32 [8], replicated, may hold values from 6 to 10
- fee_rate: float32 [8], replicated, may hold values from 0.002 to 0.02
- fund_share: float32 [120], replicated, may hold values from 0.3 to 1
- bond_flows: float32 [16384, 120], P(('pol', 'fund')), may hold values from 0.05 to 1
- bond_fund: int32 [16384], P(('pol', 'fund')), may hold values from 0 to 119, as said below
- holdings: float32 [16384], P(('pol', 'fund')), may hold values from 0.037 to 0.3
- scen_rates: float32 [3, 120, 512], P(None, None, ('parts', 'scen')), parts along dimension 2, may hold values from 0 to 0.12
Outputs:
- credited: float32 [3, 120, 512], P(None, None, ('parts', 'scen')), parts along dimension 2
- reserve: float32 [512, 32768], P(('parts', 'scen'), ('pol', 'fund')), parts along dimension 0
There are 2 independent parts, one for each index of `parts`. A program takes and returns all parts, laid end to end along the dimension named above; an argument that names none is the same for every part. Nothing has to cross between parts.
Inputs may be any that keep to these rules, and one draw needn't show every extreme that they name: `policy_fund`: every fund number appears at least once. `bond_fund`: every fund number appears at least once.
All inputs are finite; a program needn't handle non-finite values.
Results may differ from a plain program's by a relative error of at most 0.0003.
Values sent between devices are 32-bit elements; how exact they have to be, the bound alone decides.
A program may use at most 64 MiB of HBM per device.

v0:
```python
import math
import jax
import jax.numpy as jnp
from jax import lax
from jax.sharding import PartitionSpec as P

surrender_end = 84
highest = lax.Precision.HIGHEST
contract_cols = (((1,), (1,)), ((), ()))
contract_rows = (((0,), (0,)), ((), ()))


def onehot_cols(fund_ids, offset_at, breadth, fund_count):
    picked = lax.dynamic_slice_in_dim(fund_ids, offset_at, breadth, 0)
    return (lax.broadcasted_iota(jnp.int32, (fund_count, breadth), 0) == picked[None, :]).astype(
        jnp.float32
    )


def lookup(code_ids, values):
    kind_count = values.shape[0]
    matches = (
        lax.broadcasted_iota(jnp.int32, (kind_count, code_ids.shape[0]), 0) == code_ids[None, :]
    )
    return jnp.sum(jnp.where(matches, values[:, None], 0.0), axis=0)


def fund_totals(weights, fund_ids, fund_count, breadth):
    scen_rows, pol_count = weights.shape

    def add_block(block_idx, running):
        offset_at = block_idx * breadth
        onehot = onehot_cols(fund_ids, offset_at, breadth, fund_count)
        piece_blk = lax.dynamic_slice_in_dim(weights, offset_at, breadth, 1)
        return running + lax.dot_general(
            onehot, piece_blk, contract_cols, precision=highest, preferred_element_type=jnp.float32
        )

    return lax.fori_loop(
        0, pol_count // breadth, add_block, jnp.zeros((fund_count, scen_rows), jnp.float32)
    )


def advance(
    in_force,
    account,
    credited,
    market,
    lapse_pol,
    sens_pol,
    fee_pol,
    durations,
    fund_ids,
    month_idx,
    breadth,
    want_totals,
):
    fund_count = credited.shape[0]
    scen_rows, pol_count = in_force.shape

    def move_block(block_idx, carried):
        force_all, account_all, running = carried
        offset_at = block_idx * breadth
        onehot = onehot_cols(fund_ids, offset_at, breadth, fund_count)
        credit_pol = lax.dot_general(
            credited, onehot, contract_rows, precision=highest, preferred_element_type=jnp.float32
        )
        force_blk = lax.dynamic_slice_in_dim(force_all, offset_at, breadth, 1)
        account_blk = lax.dynamic_slice_in_dim(account_all, offset_at, breadth, 1)
        lapse_blk = lax.dynamic_slice_in_dim(lapse_pol, offset_at, breadth, 0)
        sens_blk = lax.dynamic_slice_in_dim(sens_pol, offset_at, breadth, 0)
        fee_blk = lax.dynamic_slice_in_dim(fee_pol, offset_at, breadth, 0)
        dur_blk = lax.dynamic_slice_in_dim(durations, offset_at, breadth, 0)
        later_mult = jnp.where(dur_blk + month_idx >= surrender_end, 2.0, 1.0)
        lapse_now = (lapse_blk * later_mult)[None, :] * jnp.exp(
            sens_blk[None, :] * (market[:, None] - credit_pol)
        )
        force_new = force_blk * jnp.exp(-lapse_now)
        account_new = account_blk * jnp.exp(credit_pol / 12.0 - fee_blk[None, :])
        force_all = lax.dynamic_update_slice_in_dim(force_all, force_new, offset_at, 1)
        account_all = lax.dynamic_update_slice_in_dim(account_all, account_new, offset_at, 1)
        if want_totals:
            running = running + lax.dot_general(
                onehot,
                force_new * account_new,
                contract_cols,
                precision=highest,
                preferred_element_type=jnp.float32,
            )
        return (force_all, account_all, running)

    return lax.fori_loop(
        0,
        pol_count // breadth,
        move_block,
        (in_force, account, jnp.zeros((fund_count, scen_rows), jnp.float32)),
    )


def local(
    count_init,
    value_init,
    durations,
    products,
    policy_fund,
    lapse_base,
    lapse_sens,
    fee_rate,
    fund_share,
    bond_flows,
    bond_fund,
    holdings,
    scen_rates,
):
    fund_count = fund_share.shape[0]
    months = scen_rates.shape[0]
    tenors = scen_rates.shape[1]
    scen_rows = scen_rates.shape[2]
    pol_count = count_init.shape[0]
    breadth = math.gcd(pol_count, 1024)
    tenor_years = (jnp.arange(tenors).astype(jnp.float32) + 1.0) / 12.0
    lapse_pol = lookup(products, lapse_base)
    sens_pol = lookup(products, lapse_sens)
    fee_pol = lookup(products, fee_rate)
    bond_onehot = onehot_cols(bond_fund, 0, bond_fund.shape[0], fund_count)

    def asset_part(month_num):
        discount = jnp.exp(-scen_rates[month_num] * tenor_years[:, None])
        bond_values = jnp.dot(
            bond_flows, discount, precision=highest, preferred_element_type=jnp.float32
        )
        return jnp.dot(
            bond_onehot,
            bond_values * holdings[:, None],
            precision=highest,
            preferred_element_type=jnp.float32,
        )

    asset_stack = lax.psum(
        jnp.stack([asset_part(month_num) for month_num in range(months)]), ("pol", "fund")
    )
    start_totals = fund_totals((count_init * value_init)[None, :], policy_fund, fund_count, breadth)
    liab_part = jnp.broadcast_to(start_totals, (fund_count, scen_rows))
    in_force = jnp.broadcast_to(count_init[None, :], (scen_rows, pol_count))
    account = jnp.broadcast_to(value_init[None, :], (scen_rows, pol_count))
    credited_list = []
    for month_idx in range(months):
        assets = asset_stack[month_idx]
        liabilities = lax.psum(liab_part, ("pol", "fund"))
        credited = fund_share[:, None] * jnp.log(assets / liabilities)
        market = scen_rates[month_idx, tenors - 1]
        in_force, account, liab_part = advance(
            in_force,
            account,
            credited,
            market,
            lapse_pol,
            sens_pol,
            fee_pol,
            durations,
            policy_fund,
            month_idx,
            breadth,
            month_idx < months - 1,
        )
        credited_list.append(credited)
    return (jnp.stack(credited_list), in_force * account)


def solution(mesh):
    in_specs = (
        P(("pol", "fund")),
        P(("pol", "fund")),
        P(("pol", "fund")),
        P(("pol", "fund")),
        P(("pol", "fund")),
        P(),
        P(),
        P(),
        P(),
        P(("pol", "fund"), None),
        P(("pol", "fund")),
        P(("pol", "fund")),
        P(None, None, ("parts", "scen")),
    )
    out_specs = (P(None, None, ("parts", "scen")), P(("parts", "scen"), ("pol", "fund")))
    return jax.shard_map(local, mesh=mesh, in_specs=in_specs, out_specs=out_specs, check_vma=False)
```

profile of v0, /device:TPU:0, one launch (start us, length us, event | category | flops | bytes accessed | tf_op | source)
XLA Modules:
  0.0 272.6 jit_solution(3409827075269828922)
XLA Ops:
  8.4 1.9 convolution_multiply_fusion
  17.2 30.9 %psum.29 = f32[120,128]{1,0:T(8,128)S(1)} all-reduce(f32[120,128]{1,0:T(8,128)S(1)} %broadcast_in_dim.151), channel_id=1, replica_groups=mesh['parts'=2,'pol'=4,'scen'=2,'fund'=2] {'pol','fund'}, use_global_device_ids=true, to_apply=%region_3.4 | all-reduce | flops 15360 | bytes 122880 | tf_op jit(solution)/shard_map/psum | solution.py:149
  48.3 24.1 %all-reduce.2.cloned.1.call-done = f32[3,120,128]{2,1,0:T(8,128)} async-done(((f32[3,120,128]{2,1,0:T(8,128)}), f32[3,120,128]{2,1,0:T(8,128)}) %all-reduce.2.cloned.1.call-update) | async-done | bytes 184336 | tf_op jit(solution)/shard_map/psum | solution.py:139
  74.0 1.9 broadcast_in_dim.153
  75.9 57.0 %while.67 = (s32[]{:T(128)}, f32[128,4096]{0,1:T(8,128)S(1)}, f32[128,4096]{0,1:T(8,128)}, f32[120,128]{1,0:T(8,128)S(1)}, f32[4096]{0:T(1024)S(1)}, /*index=5*/...) while((s32[]{:T(128)}, f32[128,4096]{0,1:T(8,128)S(1)}, ...), condition=%wide.region_8.9_spmd.clone, body=%wide.region_7.8_spmd.clone.sunk | while | flops 379995136 | bytes 21226716 | solution.py:92
  76.0 3.1 %copy.21 = f32[128,4096]{0,1:T(8,128)} copy(f32[128,4096]{0,1:T(8,128)} %get-tuple-element.1082) | data formatting | bytes 4194304 | tf_op jit(solution)/shard_map/while
  80.3 3.1 %constant_dynamic-update-slice_fusion.6 = (f32[128,4096]{0,1:T(8,128)}, f32[128,4096]{0,1:T(8,128)}, f32[1024,128]{1,0:T(8,128)}) fusion(f32[128,4096]{0,1:T(8,128)} %copy.21, s32[]{:T(128)S(6)} %select_n.110, f32[1024]{0:T(1024)S(1)} %dynamic_slice.256, f32[128,4096]{0,1:T(8,128)} %copy.22, f32[128]{0:T(128)S(1)} %bitcast.142, ...), kind=kOutput, calls=%fused_computation.27.clone.1 | convolution fusion | flops 189915136 | bytes 2699780 | tf_op jit(solution)/shard_map/while/body/eval_jaxpr/dot_general | solution.py:65
  83.5 2.0 convolution_add_fusion.4
  87.1 3.0 %copy.42 = f32[128,4096]{0,1:T(8,128)} copy(f32[128,4096]{0,1:T(8,128)} %get-tuple-element.1097) | data formatting | bytes 4194304 | tf_op jit(solution)/shard_map/while
  90.2 3.1 %copy.21 = f32[128,4096]{0,1:T(8,128)} copy(f32[128,4096]{0,1:T(8,128)} %get-tuple-element.1082) | data formatting | bytes 4194304 | tf_op jit(solution)/shard_map/while
  94.6 3.2 %constant_dynamic-update-slice_fusion.6 = (f32[128,4096]{0,1:T(8,128)}, f32[128,4096]{0,1:T(8,128)}, f32[1024,128]{1,0:T(8,128)}) fusion(f32[128,4096]{0,1:T(8,128)} %copy.21, s32[]{:T(128)S(6)} %select_n.110, f32[1024]{0:T(1024)S(1)} %dynamic_slice.256, f32[128,4096]{0,1:T(8,128)} %copy.22, f32[128]{0:T(128)S(1)} %bitcast.142, ...), kind=kOutput, calls=%fused_computation.27.clone.1 | convolution fusion | flops 189915136 | bytes 2699780 | tf_op jit(solution)/shard_map/while/body/eval_jaxpr/dot_general | solution.py:65
  97.7 2.0 convolution_add_fusion.4
  101.3 3.0 %copy.42 = f32[128,4096]{0,1:T(8,128)} copy(f32[128,4096]{0,1:T(8,128)} %get-tuple-element.1097) | data formatting | bytes 4194304 | tf_op jit(solution)/shard_map/while
  104.4 3.1 %copy.21 = f32[128,4096]{0,1:T(8,128)} copy(f32[128,4096]{0,1:T(8,128)} %get-tuple-element.1082) | data formatting | bytes 4194304 | tf_op jit(solution)/shard_map/while
  108.8 3.2 %constant_dynamic-update-slice_fusion.6 = (f32[128,4096]{0,1:T(8,128)}, f32[128,4096]{0,1:T(8,128)}, f32[1024,128]{1,0:T(8,128)}) fusion(f32[128,4096]{0,1:T(8,128)} %copy.21, s32[]{:T(128)S(6)} %select_n.110, f32[1024]{0:T(1024)S(1)} %dynamic_slice.256, f32[128,4096]{0,1:T(8,128)} %copy.22, f32[128]{0:T(128)S(1)} %bitcast.142, ...), kind=kOutput, calls=%fused_computation.27.clone.1 | convolution fusion | flops 189915136 | bytes 2699780 | tf_op jit(solution)/shard_map/while/body/eval_jaxpr/dot_general | solution.py:65
  112.0 2.0 convolution_add_fusion.4
  115.6 3.0 %copy.42 = f32[128,4096]{0,1:T(8,128)} copy(f32[128,4096]{0,1:T(8,128)} %get-tuple-element.1097) | data formatting | bytes 4194304 | tf_op jit(solution)/shard_map/while
  118.7 3.1 %copy.21 = f32[128,4096]{0,1:T(8,128)} copy(f32[128,4096]{0,1:T(8,128)} %get-tuple-element.1082) | data formatting | bytes 4194304 | tf_op jit(solution)/shard_map/while
  123.1 3.2 %constant_dynamic-update-slice_fusion.6 = (f32[128,4096]{0,1:T(8,128)}, f32[128,4096]{0,1:T(8,128)}, f32[1024,128]{1,0:T(8,128)}) fusion(f32[128,4096]{0,1:T(8,128)} %copy.21, s32[]{:T(128)S(6)} %select_n.110, f32[1024]{0:T(1024)S(1)} %dynamic_slice.256, f32[128,4096]{0,1:T(8,128)} %copy.22, f32[128]{0:T(128)S(1)} %bitcast.142, ...), kind=kOutput, calls=%fused_computation.27.clone.1 | convolution fusion | flops 189915136 | bytes 2699780 | tf_op jit(solution)/shard_map/while/body/eval_jaxpr/dot_general | solution.py:65
  126.2 2.0 convolution_add_fusion.4
  129.8 3.0 %copy.42 = f32[128,4096]{0,1:T(8,128)} copy(f32[128,4096]{0,1:T(8,128)} %get-tuple-element.1097) | data formatting | bytes 4194304 | tf_op jit(solution)/shard_map/while
  132.9 27.7 %psum.30 = f32[120,128]{1,0:T(8,128)S(1)} all-reduce(f32[120,128]{1,0:T(8,128)S(1)} %get-tuple-element.624), channel_id=1, replica_groups=mesh['parts'=2,'pol'=4,'scen'=2,'fund'=2] {'pol','fund'}, use_global_device_ids=true, to_apply=%region_9.10 | all-reduce | flops 15360 | bytes 122880 | tf_op jit(solution)/shard_map/psum | solution.py:149
  161.6 57.0 %while.68 = (s32[]{:T(128)}, f32[128,4096]{0,1:T(8,128)S(1)}, f32[128,4096]{0,1:T(8,128)}, f32[120,128]{1,0:T(8,128)S(1)}, f32[4096]{0:T(1024)S(1)}, /*index=5*/...) while((s32[]{:T(128)}, f32[128,4096]{0,1:T(8,128)S(1)}, ...), condition=%wide.region_11.12_spmd.clone, body=%wide.region_10.11_spmd.clone.sunk | while | flops 379996160 | bytes 21226716 | solution.py:92
  161.6 3.1 %copy.23 = f32[128,4096]{0,1:T(8,128)} copy(f32[128,4096]{0,1:T(8,128)} %get-tuple-element.1127) | data formatting | bytes 4194304 | tf_op jit(solution)/shard_map/while
  166.0 3.1 %constant_dynamic-update-slice_fusion.7 = (f32[128,4096]{0,1:T(8,128)}, f32[128,4096]{0,1:T(8,128)}, f32[1024,128]{1,0:T(8,128)}) fusion(f32[128,4096]{0,1:T(8,128)} %copy.23, s32[]{:T(128)S(6)} %select_n.112, f32[1024]{0:T(1024)S(1)} %dynamic_slice.264, f32[128,4096]{0,1:T(8,128)} %copy.24, f32[128]{0:T(128)S(1)} %bitcast.140, ...), kind=kOutput, calls=%fused_computation.39.clone.1 | convolution fusion | flops 189915136 | bytes 2699780 | tf_op jit(solution)/shard_map/while/body/eval_jaxpr/dot_general | solution.py:65
  169.2 2.0 convolution_add_fusion.5
  172.8 3.0 %copy.54 = f32[128,4096]{0,1:T(8,128)} copy(f32[128,4096]{0,1:T(8,128)} %get-tuple-element.1142) | data formatting | bytes 4194304 | tf_op jit(solution)/shard_map/while
  175.9 3.1 %copy.23 = f32[128,4096]{0,1:T(8,128)} copy(f32[128,4096]{0,1:T(8,128)} %get-tuple-element.1127) | data formatting | bytes 4194304 | tf_op jit(solution)/shard_map/while
  180.2 3.2 %constant_dynamic-update-slice_fusion.7 = (f32[128,4096]{0,1:T(8,128)}, f32[128,4096]{0,1:T(8,128)}, f32[1024,128]{1,0:T(8,128)}) fusion(f32[128,4096]{0,1:T(8,128)} %copy.23, s32[]{:T(128)S(6)} %select_n.112, f32[1024]{0:T(1024)S(1)} %dynamic_slice.264, f32[128,4096]{0,1:T(8,128)} %copy.24, f32[128]{0:T(128)S(1)} %bitcast.140, ...), kind=kOutput, calls=%fused_computation.39.clone.1 | convolution fusion | flops 189915136 | bytes 2699780 | tf_op jit(solution)/shard_map/while/body/eval_jaxpr/dot_general | solution.py:65
  183.4 2.0 convolution_add_fusion.5
  187.0 3.0 %copy.54 = f32[128,4096]{0,1:T(8,128)} copy(f32[128,4096]{0,1:T(8,128)} %get-tuple-element.1142) | data formatting | bytes 4194304 | tf_op jit(solution)/shard_map/while
  190.1 3.1 %copy.23 = f32[128,4096]{0,1:T(8,128)} copy(f32[128,4096]{0,1:T(8,128)} %get-tuple-element.1127) | data formatting | bytes 4194304 | tf_op jit(solution)/shard_map/while
  194.5 3.2 %constant_dynamic-update-slice_fusion.7 = (f32[128,4096]{0,1:T(8,128)}, f32[128,4096]{0,1:T(8,128)}, f32[1024,128]{1,0:T(8,128)}) fusion(f32[128,4096]{0,1:T(8,128)} %copy.23, s32[]{:T(128)S(6)} %select_n.112, f32[1024]{0:T(1024)S(1)} %dynamic_slice.264, f32[128,4096]{0,1:T(8,128)} %copy.24, f32[128]{0:T(128)S(1)} %bitcast.140, ...), kind=kOutput, calls=%fused_computation.39.clone.1 | convolution fusion | flops 189915136 | bytes 2699780 | tf_op jit(solution)/shard_map/while/body/eval_jaxpr/dot_general | solution.py:65
  197.7 2.0 convolution_add_fusion.5
  201.3 3.0 %copy.54 = f32[128,4096]{0,1:T(8,128)} copy(f32[128,4096]{0,1:T(8,128)} %get-tuple-element.1142) | data formatting | bytes 4194304 | tf_op jit(solution)/shard_map/while
  204.3 3.1 %copy.23 = f32[128,4096]{0,1:T(8,128)} copy(f32[128,4096]{0,1:T(8,128)} %get-tuple-element.1127) | data formatting | bytes 4194304 | tf_op jit(solution)/shard_map/while
  208.7 3.2 %constant_dynamic-update-slice_fusion.7 = (f32[128,4096]{0,1:T(8,128)}, f32[128,4096]{0,1:T(8,128)}, f32[1024,128]{1,0:T(8,128)}) fusion(f32[128,4096]{0,1:T(8,128)} %copy.23, s32[]{:T(128)S(6)} %select_n.112, f32[1024]{0:T(1024)S(1)} %dynamic_slice.264, f32[128,4096]{0,1:T(8,128)} %copy.24, f32[128]{0:T(128)S(1)} %bitcast.140, ...), kind=kOutput, calls=%fused_computation.39.clone.1 | convolution fusion | flops 189915136 | bytes 2699780 | tf_op jit(solution)/shard_map/while/body/eval_jaxpr/dot_general | solution.py:65
  211.9 2.0 convolution_add_fusion.5
  215.5 3.0 %copy.54 = f32[128,4096]{0,1:T(8,128)} copy(f32[128,4096]{0,1:T(8,128)} %get-tuple-element.1142) | data formatting | bytes 4194304 | tf_op jit(solution)/shard_map/while
  218.6 26.4 %psum.31 = f32[120,128]{1,0:T(8,128)S(1)} all-reduce(f32[120,128]{1,0:T(8,128)S(1)} %get-tuple-element.627), channel_id=1, replica_groups=mesh['parts'=2,'pol'=4,'scen'=2,'fund'=2] {'pol','fund'}, use_global_device_ids=true, to_apply=%region_12.13 | all-reduce | flops 15360 | bytes 122880 | tf_op jit(solution)/shard_map/psum | solution.py:149
  245.8 11.2 %while.65 = (s32[]{:T(128)}, f32[128,4096]{0,1:T(8,128)S(1)}, f32[128,4096]{0,1:T(8,128)}, f32[4096]{0:T(1024)S(1)}, s32[4096]{0:T(1024)S(1)}, /*index=5*/f32[40...) while((s32[]{:T(128)}, f32[128,4096]{0,1:T(8,128)S(1)}, ...), condition=%wide.region_14.15_spmd, body=%wide.region_13.14_spmd.sunk | while | flops 189919232 | bytes 2212551 | solution.py:92
  245.9 2.8 %fusion.63 = (f32[128,4096]{0,1:T(8,128)}, f32[128,4096]{0,1:T(8,128)S(1)}) fusion(f32[128,4096]{0,1:T(8,128)} %get-tuple-element.1171, s32[]{:T(128)S(6)} %select_n.107, f32[1024]{0:T(1024)S(1)} %dynamic_slice.246, f32[128,4096]{0,1:T(8,128)S(1)} %get-tuple-element.1170, f32[128]{0:T(128)S(1)} %bitcast.144, f32[1024]{0:T(1024)S(1)} %dynamic_slice.247, ...), kind=kOutput, calls=%fused_computation.1.clone.1 | convolution fusion | flops 189915136 | bytes 2175492 | tf_op jit(solution)/shard_map/while/body/eval_jaxpr/dot_general | solution.py:65
  248.7 2.8 %fusion.63 = (f32[128,4096]{0,1:T(8,128)}, f32[128,4096]{0,1:T(8,128)S(1)}) fusion(f32[128,4096]{0,1:T(8,128)} %get-tuple-element.1171, s32[]{:T(128)S(6)} %select_n.107, f32[1024]{0:T(1024)S(1)} %dynamic_slice.246, f32[128,4096]{0,1:T(8,128)S(1)} %get-tuple-element.1170, f32[128]{0:T(128)S(1)} %bitcast.144, f32[1024]{0:T(1024)S(1)} %dynamic_slice.247, ...), kind=kOutput, calls=%fused_computation.1.clone.1 | convolution fusion | flops 189915136 | bytes 2175492 | tf_op jit(solution)/shard_map/while/body/eval_jaxpr/dot_general | solution.py:65
  251.5 2.8 %fusion.63 = (f32[128,4096]{0,1:T(8,128)}, f32[128,4096]{0,1:T(8,128)S(1)}) fusion(f32[128,4096]{0,1:T(8,128)} %get-tuple-element.1171, s32[]{:T(128)S(6)} %select_n.107, f32[1024]{0:T(1024)S(1)} %dynamic_slice.246, f32[128,4096]{0,1:T(8,128)S(1)} %get-tuple-element.1170, f32[128]{0:T(128)S(1)} %bitcast.144, f32[1024]{0:T(1024)S(1)} %dynamic_slice.247, ...), kind=kOutput, calls=%fused_computation.1.clone.1 | convolution fusion | flops 189915136 | bytes 2175492 | tf_op jit(solution)/shard_map/while/body/eval_jaxpr/dot_general | solution.py:65
  254.3 2.8 %fusion.63 = (f32[128,4096]{0,1:T(8,128)}, f32[128,4096]{0,1:T(8,128)S(1)}) fusion(f32[128,4096]{0,1:T(8,128)} %get-tuple-element.1171, s32[]{:T(128)S(6)} %select_n.107, f32[1024]{0:T(1024)S(1)} %dynamic_slice.246, f32[128,4096]{0,1:T(8,128)S(1)} %get-tuple-element.1170, f32[128]{0:T(128)S(1)} %bitcast.144, f32[1024]{0:T(1024)S(1)} %dynamic_slice.247, ...), kind=kOutput, calls=%fused_computation.1.clone.1 | convolution fusion | flops 189915136 | bytes 2175492 | tf_op jit(solution)/shard_map/while/body/eval_jaxpr/dot_general | solution.py:65
  257.1 1.8 copy.17
  258.9 3.0 %copy.18 = f32[128,4096]{1,0:T(8,128)} copy(f32[128,4096]{0,1:T(8,128)} %get-tuple-element.631) | data formatting | bytes 4194304 | tf_op jit(solution)/shard_map/while | solution.py:92
  261.9 3.1 %mul.323 = f32[128,4096]{1,0:T(8,128)} multiply(f32[128,4096]{1,0:T(8,128)S(1)} %copy-done.1, f32[128,4096]{1,0:T(8,128)} %copy.18) | non-fusion elementwise | flops 524288 | bytes 6291456 | tf_op jit(solution)/shard_map/mul | solution.py:167
  (122 shorter events, 36.7 us)
Async XLA Ops:
  7.2 1.2 copy-start
  7.2 3.1 %copy-start.5 = (f32[2048]{0:T(1024)S(1)}, f32[2048]{0:T(1024)}, u32[]{:S(2)}) copy-start(f32[2048]{0:T(1024)} %param.32) | copy-start | bytes 24580
  7.2 3.1 %copy-start.4 = (f32[3,120,128]{2,1,0:T(8,128)S(1)}, f32[3,120,128]{2,1,0:T(8,128)}, u32[]{:S(2)}) copy-start(f32[3,120,128]{2,1,0:T(8,128)} %param.33) | copy-start | bytes 552964
  7.2 65.3 %all-reduce.2.cloned.1.call-start = ((), (), s32[]{:S(2)}) async-start(), calls=%async_computation | async-start | bytes 368640 | tf_op jit(solution)/shard_map/psum | solution.py:139
  10.3 2.2 copy-start.6
  12.6 3.1 %copy-start.7 = (f32[4096]{0:T(1024)S(1)}, f32[4096]{0:T(1024)}, u32[]{:S(2)}) copy-start(f32[4096]{0:T(1024)} %param.21) | copy-start | bytes 49156
  12.6 3.1 %copy-start.8 = (f32[4096]{0:T(1024)S(1)}, f32[4096]{0:T(1024)}, u32[]{:S(2)}) copy-start(f32[4096]{0:T(1024)} %param.22) | copy-start | bytes 49156
  12.6 3.1 %copy-start.2 = (s32[4096]{0:T(1024)S(1)}, s32[4096]{0:T(1024)}, u32[]{:S(2)}) copy-start(s32[4096]{0:T(1024)} %param.25) | copy-start | bytes 49156
  13.4 34.8 %copy-start.9 = (s32[4096]{0:T(1024)S(1)}, s32[4096]{0:T(1024)}, u32[]{:S(2)}) copy-start(s32[4096]{0:T(1024)} %param.24) | copy-start | bytes 49156
  13.4 34.7 %copy-start.11 = (f32[8]{0:T(128)S(1)}, f32[8]{0:T(128)}, u32[]{:S(2)}) copy-start(f32[8]{0:T(128)} %param.28) | copy-start | bytes 100
  13.4 34.7 %copy-start.12 = (f32[8]{0:T(128)S(1)}, f32[8]{0:T(128)}, u32[]{:S(2)}) copy-start(f32[8]{0:T(128)} %param.27) | copy-start | bytes 100
  13.4 34.7 %copy-start.13 = (f32[8]{0:T(128)S(1)}, f32[8]{0:T(128)}, u32[]{:S(2)}) copy-start(f32[8]{0:T(128)} %param.26) | copy-start | bytes 100
  13.4 59.0 %copy-start.10 = (f32[120]{0:T(128)S(1)}, f32[120]{0:T(128)}, u32[]{:S(2)}) copy-start(f32[120]{0:T(128)} %param.29) | copy-start | bytes 1444
  73.4 2.5 copy-start.3
  258.9 3.0 %copy-start.1 = (f32[128,4096]{1,0:T(8,128)S(1)}, f32[128,4096]{1,0:T(8,128)}, u32[]{:S(2)}) copy-start(f32[128,4096]{1,0:T(8,128)} %copy.17) | copy-start | bytes 6291460
Sparse Core Ops, SparseCore 0:
  15.8 56.6 all-reduce.1
where the time goes:
time: 274 us; the launch traced here: 273 us
  blocking collectives  85 us (31%)
  local copies, waits for them, and re-layouts  81 us (30%)
  matrix products  60 us (22%)
  waiting for transfers between devices  24.1 us (9%)
  between operations  14.4 us (5%)
  other arithmetic  7.53 us (3%)
    psum x3, blocking collectives, local(): liabilities = lax.psum(liab_part, ('pol', 'fund'))  85 us
    while x32, local copies, waits for them, and re-layouts  72 us
    dot_general x12, matrix products, move_block(): lax.dot_general(credited, onehot, contract_rows, precision=highest, prefe...  36.4 us
    psum x1, waiting for transfers between devices, local(): lax.psum(jnp.stack([asset_part(month_num) for month_num in range(months)]...  24.1 us
    dot_general x8, matrix products, move_block(): lax.dot_general(onehot, force_new * account_new, contract_cols, precision...  16.2 us
  transfers between devices with their start and end apart: 1, of which 1 were waited for; matrix products, arithmetic and copies ran while one was open for 1% of the time, Pallas kernels for 0%

commit v1 on v0

--- a/solution.py
+++ b/solution.py
@@ -146,7 +146,8 @@
     credited_list = []
     for month_idx in range(months):
         assets = asset_stack[month_idx]
-        liabilities = lax.psum(liab_part, ("pol", "fund"))
+        inner = lax.psum(liab_part, "fund")
+        liabilities = lax.psum(inner, "pol")
         credited = fund_share[:, None] * jnp.log(assets / liabilities)
         market = scen_rates[month_idx, tenors - 1]
         in_force, account, liab_part = advance(

time: 274 us -> 263 us (0.960)
  blocking collectives: 85 us -> 67.8 us
  waiting for transfers between devices: 24.1 us -> 30.2 us
    psum x3 -> x6, blocking collectives: 85 us -> 67.8 us  [the longest x3 56.7 us: local(): liabilities = lax.psum(inner, 'pol')]
    psum x1, waiting for transfers between devices: 24.1 us -> 30.2 us  [local(): lax.psum(jnp.stack([asset_part(month_num) for month_num in range(months)]...]
where the time goes in v1:
time: 263 us; the launch traced here: 262 us
  local copies, waits for them, and re-layouts  81.1 us (31%)
  blocking collectives  67.8 us (26%)
  matrix products  60 us (23%)
  waiting for transfers between devices  30.2 us (11%)
  between operations  14.4 us (5%)
  other arithmetic  7.57 us (3%)
    while x32, local copies, waits for them, and re-layouts  72.1 us
    psum x3, blocking collectives, local(): liabilities = lax.psum(inner, 'pol')  56.7 us
    dot_general x12, matrix products, move_block(): lax.dot_general(credited, onehot, contract_rows, precision=highest, prefe...  36.4 us
    psum x1, waiting for transfers between devices, local(): lax.psum(jnp.stack([asset_part(month_num) for month_num in range(months)]...  30.2 us
    dot_general x8, matrix products, move_block(): lax.dot_general(onehot, force_new * account_new, contract_cols, precision...  16.2 us
    psum x3, blocking collectives, local(): inner = lax.psum(liab_part, 'fund')  11.1 us
  transfers between devices with their start and end apart: 1, of which 1 were waited for; matrix products, arithmetic and copies ran while one was open for 1% of the time, Pallas kernels for 0%

profile of v1, /device:TPU:0, one launch (start us, length us, event | category | flops | bytes accessed | tf_op | source)
XLA Modules:
  0.0 261.7 jit_solution(2698670872480252246)
XLA Ops:
  17.2 3.9 %psum.50 = f32[120,128]{1,0:T(8,128)S(1)} all-reduce(f32[120,128]{1,0:T(8,128)S(1)} %broadcast_in_dim.151), channel_id=1, replica_groups=mesh['parts'=2,'pol'=4,'scen'=2,'fund'=2] {'fund'}, use_global_device_ids=true, to_apply=%region_3.4 | all-reduce | flops 15360 | bytes 122880 | tf_op jit(solution)/shard_map/psum | solution.py:149
  21.2 21.1 %psum.51 = f32[120,128]{1,0:T(8,128)S(1)} all-reduce(f32[120,128]{1,0:T(8,128)S(1)} %psum.50), channel_id=1, replica_groups=mesh['parts'=2,'pol'=4,'scen'=2,'fund'=2] {'pol'}, use_global_device_ids=true, to_apply=%region_4.5 | all-reduce | flops 15360 | bytes 122880 | tf_op jit(solution)/shard_map/psum | solution.py:150
  42.5 30.2 %all-reduce.2.cloned.1.call-done = f32[3,120,128]{2,1,0:T(8,128)} async-done(((f32[3,120,128]{2,1,0:T(8,128)}), f32[3,120,128]{2,1,0:T(8,128)}) %all-reduce.2.cloned.1.call-update) | async-done | bytes 184336 | tf_op jit(solution)/shard_map/psum | solution.py:139
  76.2 57.0 %while.67 = (s32[]{:T(128)}, f32[128,4096]{0,1:T(8,128)S(1)}, f32[128,4096]{0,1:T(8,128)}, f32[120,128]{1,0:T(8,128)S(1)}, f32[4096]{0:T(1024)S(1)}, /*index=5*/...) while((s32[]{:T(128)}, f32[128,4096]{0,1:T(8,128)S(1)}, ...), condition=%wide.region_9.10_spmd.clone, body=%wide.region_8.9_spmd.clone.sunk | while | flops 379995136 | bytes 21226716 | solution.py:92
  76.3 3.1 %copy.21 = f32[128,4096]{0,1:T(8,128)} copy(f32[128,4096]{0,1:T(8,128)} %get-tuple-element.1082) | data formatting | bytes 4194304 | tf_op jit(solution)/shard_map/while
  80.7 3.1 %constant_dynamic-update-slice_fusion.6 = (f32[128,4096]{0,1:T(8,128)}, f32[128,4096]{0,1:T(8,128)}, f32[1024,128]{1,0:T(8,128)}) fusion(f32[128,4096]{0,1:T(8,128)} %copy.21, s32[]{:T(128)S(6)} %select_n.110, f32[1024]{0:T(1024)S(1)} %dynamic_slice.256, f32[128,4096]{0,1:T(8,128)} %copy.22, f32[128]{0:T(128)S(1)} %bitcast.142, ...), kind=kOutput, calls=%fused_computation.27.clone.1 | convolution fusion | flops 189915136 | bytes 2699780 | tf_op jit(solution)/shard_map/while/body/eval_jaxpr/dot_general | solution.py:65
  83.8 2.0 convolution_add_fusion.4
  87.4 3.0 %copy.42 = f32[128,4096]{0,1:T(8,128)} copy(f32[128,4096]{0,1:T(8,128)} %get-tuple-element.1097) | data formatting | bytes 4194304 | tf_op jit(solution)/shard_map/while
  90.5 3.1 %copy.21 = f32[128,4096]{0,1:T(8,128)} copy(f32[128,4096]{0,1:T(8,128)} %get-tuple-element.1082) | data formatting | bytes 4194304 | tf_op jit(solution)/shard_map/while
  94.9 3.2 %constant_dynamic-update-slice_fusion.6 = (f32[128,4096]{0,1:T(8,128)}, f32[128,4096]{0,1:T(8,128)}, f32[1024,128]{1,0:T(8,128)}) fusion(f32[128,4096]{0,1:T(8,128)} %copy.21, s32[]{:T(128)S(6)} %select_n.110, f32[1024]{0:T(1024)S(1)} %dynamic_slice.256, f32[128,4096]{0,1:T(8,128)} %copy.22, f32[128]{0:T(128)S(1)} %bitcast.142, ...), kind=kOutput, calls=%fused_computation.27.clone.1 | convolution fusion | flops 189915136 | bytes 2699780 | tf_op jit(solution)/shard_map/while/body/eval_jaxpr/dot_general | solution.py:65
  98.0 2.0 convolution_add_fusion.4
  101.7 3.0 %copy.42 = f32[128,4096]{0,1:T(8,128)} copy(f32[128,4096]{0,1:T(8,128)} %get-tuple-element.1097) | data formatting | bytes 4194304 | tf_op jit(solution)/shard_map/while
  104.7 3.1 %copy.21 = f32[128,4096]{0,1:T(8,128)} copy(f32[128,4096]{0,1:T(8,128)} %get-tuple-element.1082) | data formatting | bytes 4194304 | tf_op jit(solution)/shard_map/while
  109.1 3.2 %constant_dynamic-update-slice_fusion.6 = (f32[128,4096]{0,1:T(8,128)}, f32[128,4096]{0,1:T(8,128)}, f32[1024,128]{1,0:T(8,128)}) fusion(f32[128,4096]{0,1:T(8,128)} %copy.21, s32[]{:T(128)S(6)} %select_n.110, f32[1024]{0:T(1024)S(1)} %dynamic_slice.256, f32[128,4096]{0,1:T(8,128)} %copy.22, f32[128]{0:T(128)S(1)} %bitcast.142, ...), kind=kOutput, calls=%fused_computation.27.clone.1 | convolution fusion | flops 189915136 | bytes 2699780 | tf_op jit(solution)/shard_map/while/body/eval_jaxpr/dot_general | solution.py:65
  112.3 2.0 convolution_add_fusion.4
  115.9 3.0 %copy.42 = f32[128,4096]{0,1:T(8,128)} copy(f32[128,4096]{0,1:T(8,128)} %get-tuple-element.1097) | data formatting | bytes 4194304 | tf_op jit(solution)/shard_map/while
  119.0 3.1 %copy.21 = f32[128,4096]{0,1:T(8,128)} copy(f32[128,4096]{0,1:T(8,128)} %get-tuple-element.1082) | data formatting | bytes 4194304 | tf_op jit(solution)/shard_map/while
  123.4 3.2 %constant_dynamic-update-slice_fusion.6 = (f32[128,4096]{0,1:T(8,128)}, f32[128,4096]{0,1:T(8,128)}, f32[1024,128]{1,0:T(8,128)}) fusion(f32[128,4096]{0,1:T(8,128)} %copy.21, s32[]{:T(128)S(6)} %select_n.110, f32[1024]{0:T(1024)S(1)} %dynamic_slice.256, f32[128,4096]{0,1:T(8,128)} %copy.22, f32[128]{0:T(128)S(1)} %bitcast.142, ...), kind=kOutput, calls=%fused_computation.27.clone.1 | convolution fusion | flops 189915136 | bytes 2699780 | tf_op jit(solution)/shard_map/while/body/eval_jaxpr/dot_general | solution.py:65
  126.6 2.0 convolution_add_fusion.4
  130.2 3.0 %copy.42 = f32[128,4096]{0,1:T(8,128)} copy(f32[128,4096]{0,1:T(8,128)} %get-tuple-element.1097) | data formatting | bytes 4194304 | tf_op jit(solution)/shard_map/while
  133.2 3.6 %psum.52 = f32[120,128]{1,0:T(8,128)S(1)} all-reduce(f32[120,128]{1,0:T(8,128)S(1)} %get-tuple-element.624), channel_id=1, replica_groups=mesh['parts'=2,'pol'=4,'scen'=2,'fund'=2] {'fund'}, use_global_device_ids=true, to_apply=%region_10.11 | all-reduce | flops 15360 | bytes 122880 | tf_op jit(solution)/shard_map/psum | solution.py:149
  136.8 19.2 %psum.53 = f32[120,128]{1,0:T(8,128)S(1)} all-reduce(f32[120,128]{1,0:T(8,128)S(1)} %psum.52), channel_id=1, replica_groups=mesh['parts'=2,'pol'=4,'scen'=2,'fund'=2] {'pol'}, use_global_device_ids=true, to_apply=%region_11.12 | all-reduce | flops 15360 | bytes 122880 | tf_op jit(solution)/shard_map/psum | solution.py:150
  156.9 57.0 %while.68 = (s32[]{:T(128)}, f32[128,4096]{0,1:T(8,128)S(1)}, f32[128,4096]{0,1:T(8,128)}, f32[120,128]{1,0:T(8,128)S(1)}, f32[4096]{0:T(1024)S(1)}, /*index=5*/...) while((s32[]{:T(128)}, f32[128,4096]{0,1:T(8,128)S(1)}, ...), condition=%wide.region_13.14_spmd.clone, body=%wide.region_12.13_spmd.clone.sunk | while | flops 379996160 | bytes 21226716 | solution.py:92
  157.0 3.1 %copy.23 = f32[128,4096]{0,1:T(8,128)} copy(f32[128,4096]{0,1:T(8,128)} %get-tuple-element.1127) | data formatting | bytes 4194304 | tf_op jit(solution)/shard_map/while
  161.4 3.1 %constant_dynamic-update-slice_fusion.7 = (f32[128,4096]{0,1:T(8,128)}, f32[128,4096]{0,1:T(8,128)}, f32[1024,128]{1,0:T(8,128)}) fusion(f32[128,4096]{0,1:T(8,128)} %copy.23, s32[]{:T(128)S(6)} %select_n.112, f32[1024]{0:T(1024)S(1)} %dynamic_slice.264, f32[128,4096]{0,1:T(8,128)} %copy.24, f32[128]{0:T(128)S(1)} %bitcast.140, ...), kind=kOutput, calls=%fused_computation.39.clone.1 | convolution fusion | flops 189915136 | bytes 2699780 | tf_op jit(solution)/shard_map/while/body/eval_jaxpr/dot_general | solution.py:65
  164.5 2.0 convolution_add_fusion.5
  168.2 3.0 %copy.54 = f32[128,4096]{0,1:T(8,128)} copy(f32[128,4096]{0,1:T(8,128)} %get-tuple-element.1142) | data formatting | bytes 4194304 | tf_op jit(solution)/shard_map/while
  171.2 3.1 %copy.23 = f32[128,4096]{0,1:T(8,128)} copy(f32[128,4096]{0,1:T(8,128)} %get-tuple-element.1127) | data formatting | bytes 4194304 | tf_op jit(solution)/shard_map/while
  175.6 3.2 %constant_dynamic-update-slice_fusion.7 = (f32[128,4096]{0,1:T(8,128)}, f32[128,4096]{0,1:T(8,128)}, f32[1024,128]{1,0:T(8,128)}) fusion(f32[128,4096]{0,1:T(8,128)} %copy.23, s32[]{:T(128)S(6)} %select_n.112, f32[1024]{0:T(1024)S(1)} %dynamic_slice.264, f32[128,4096]{0,1:T(8,128)} %copy.24, f32[128]{0:T(128)S(1)} %bitcast.140, ...), kind=kOutput, calls=%fused_computation.39.clone.1 | convolution fusion | flops 189915136 | bytes 2699780 | tf_op jit(solution)/shard_map/while/body/eval_jaxpr/dot_general | solution.py:65
  178.8 2.0 convolution_add_fusion.5
  182.4 3.0 %copy.54 = f32[128,4096]{0,1:T(8,128)} copy(f32[128,4096]{0,1:T(8,128)} %get-tuple-element.1142) | data formatting | bytes 4194304 | tf_op jit(solution)/shard_map/while
  185.5 3.1 %copy.23 = f32[128,4096]{0,1:T(8,128)} copy(f32[128,4096]{0,1:T(8,128)} %get-tuple-element.1127) | data formatting | bytes 4194304 | tf_op jit(solution)/shard_map/while
  189.8 3.2 %constant_dynamic-update-slice_fusion.7 = (f32[128,4096]{0,1:T(8,128)}, f32[128,4096]{0,1:T(8,128)}, f32[1024,128]{1,0:T(8,128)}) fusion(f32[128,4096]{0,1:T(8,128)} %copy.23, s32[]{:T(128)S(6)} %select_n.112, f32[1024]{0:T(1024)S(1)} %dynamic_slice.264, f32[128,4096]{0,1:T(8,128)} %copy.24, f32[128]{0:T(128)S(1)} %bitcast.140, ...), kind=kOutput, calls=%fused_computation.39.clone.1 | convolution fusion | flops 189915136 | bytes 2699780 | tf_op jit(solution)/shard_map/while/body/eval_jaxpr/dot_general | solution.py:65
  193.0 2.0 convolution_add_fusion.5
  196.7 3.0 %copy.54 = f32[128,4096]{0,1:T(8,128)} copy(f32[128,4096]{0,1:T(8,128)} %get-tuple-element.1142) | data formatting | bytes 4194304 | tf_op jit(solution)/shard_map/while
  199.7 3.1 %copy.23 = f32[128,4096]{0,1:T(8,128)} copy(f32[128,4096]{0,1:T(8,128)} %get-tuple-element.1127) | data formatting | bytes 4194304 | tf_op jit(solution)/shard_map/while
  204.1 3.2 %constant_dynamic-update-slice_fusion.7 = (f32[128,4096]{0,1:T(8,128)}, f32[128,4096]{0,1:T(8,128)}, f32[1024,128]{1,0:T(8,128)}) fusion(f32[128,4096]{0,1:T(8,128)} %copy.23, s32[]{:T(128)S(6)} %select_n.112, f32[1024]{0:T(1024)S(1)} %dynamic_slice.264, f32[128,4096]{0,1:T(8,128)} %copy.24, f32[128]{0:T(128)S(1)} %bitcast.140, ...), kind=kOutput, calls=%fused_computation.39.clone.1 | convolution fusion | flops 189915136 | bytes 2699780 | tf_op jit(solution)/shard_map/while/body/eval_jaxpr/dot_general | solution.py:65
  207.3 2.0 convolution_add_fusion.5
  210.9 3.0 %copy.54 = f32[128,4096]{0,1:T(8,128)} copy(f32[128,4096]{0,1:T(8,128)} %get-tuple-element.1142) | data formatting | bytes 4194304 | tf_op jit(solution)/shard_map/while
  214.0 3.6 %psum.54 = f32[120,128]{1,0:T(8,128)S(1)} all-reduce(f32[120,128]{1,0:T(8,128)S(1)} %get-tuple-element.627), channel_id=1, replica_groups=mesh['parts'=2,'pol'=4,'scen'=2,'fund'=2] {'fund'}, use_global_device_ids=true, to_apply=%region_14.15 | all-reduce | flops 15360 | bytes 122880 | tf_op jit(solution)/shard_map/psum | solution.py:149
  217.5 16.4 %psum.55 = f32[120,128]{1,0:T(8,128)S(1)} all-reduce(f32[120,128]{1,0:T(8,128)S(1)} %psum.54), channel_id=1, replica_groups=mesh['parts'=2,'pol'=4,'scen'=2,'fund'=2] {'pol'}, use_global_device_ids=true, to_apply=%region_15.16 | all-reduce | flops 15360 | bytes 122880 | tf_op jit(solution)/shard_map/psum | solution.py:150
  234.9 11.2 %while.65 = (s32[]{:T(128)}, f32[128,4096]{0,1:T(8,128)S(1)}, f32[128,4096]{0,1:T(8,128)}, f32[4096]{0:T(1024)S(1)}, s32[4096]{0:T(1024)S(1)}, /*index=5*/f32[40...) while((s32[]{:T(128)}, f32[128,4096]{0,1:T(8,128)S(1)}, ...), condition=%wide.region_17.18_spmd, body=%wide.region_16.17_spmd.sunk | while | flops 189919232 | bytes 2212551 | solution.py:92
  235.0 2.8 %fusion.63 = (f32[128,4096]{0,1:T(8,128)}, f32[128,4096]{0,1:T(8,128)S(1)}) fusion(f32[128,4096]{0,1:T(8,128)} %get-tuple-element.1171, s32[]{:T(128)S(6)} %select_n.107, f32[1024]{0:T(1024)S(1)} %dynamic_slice.246, f32[128,4096]{0,1:T(8,128)S(1)} %get-tuple-element.1170, f32[128]{0:T(128)S(1)} %bitcast.144, f32[1024]{0:T(1024)S(1)} %dynamic_slice.247, ...), kind=kOutput, calls=%fused_computation.1.clone.1 | convolution fusion | flops 189915136 | bytes 2175492 | tf_op jit(solution)/shard_map/while/body/eval_jaxpr/dot_general | solution.py:65
  237.8 2.8 %fusion.63 = (f32[128,4096]{0,1:T(8,128)}, f32[128,4096]{0,1:T(8,128)S(1)}) fusion(f32[128,4096]{0,1:T(8,128)} %get-tuple-element.1171, s32[]{:T(128)S(6)} %select_n.107, f32[1024]{0:T(1024)S(1)} %dynamic_slice.246, f32[128,4096]{0,1:T(8,128)S(1)} %get-tuple-element.1170, f32[128]{0:T(128)S(1)} %bitcast.144, f32[1024]{0:T(1024)S(1)} %dynamic_slice.247, ...), kind=kOutput, calls=%fused_computation.1.clone.1 | convolution fusion | flops 189915136 | bytes 2175492 | tf_op jit(solution)/shard_map/while/body/eval_jaxpr/dot_general | solution.py:65
  240.6 2.8 %fusion.63 = (f32[128,4096]{0,1:T(8,128)}, f32[128,4096]{0,1:T(8,128)S(1)}) fusion(f32[128,4096]{0,1:T(8,128)} %get-tuple-element.1171, s32[]{:T(128)S(6)} %select_n.107, f32[1024]{0:T(1024)S(1)} %dynamic_slice.246, f32[128,4096]{0,1:T(8,128)S(1)} %get-tuple-element.1170, f32[128]{0:T(128)S(1)} %bitcast.144, f32[1024]{0:T(1024)S(1)} %dynamic_slice.247, ...), kind=kOutput, calls=%fused_computation.1.clone.1 | convolution fusion | flops 189915136 | bytes 2175492 | tf_op jit(solution)/shard_map/while/body/eval_jaxpr/dot_general | solution.py:65
  243.3 2.8 %fusion.63 = (f32[128,4096]{0,1:T(8,128)}, f32[128,4096]{0,1:T(8,128)S(1)}) fusion(f32[128,4096]{0,1:T(8,128)} %get-tuple-element.1171, s32[]{:T(128)S(6)} %select_n.107, f32[1024]{0:T(1024)S(1)} %dynamic_slice.246, f32[128,4096]{0,1:T(8,128)S(1)} %get-tuple-element.1170, f32[128]{0:T(128)S(1)} %bitcast.144, f32[1024]{0:T(1024)S(1)} %dynamic_slice.247, ...), kind=kOutput, calls=%fused_computation.1.clone.1 | convolution fusion | flops 189915136 | bytes 2175492 | tf_op jit(solution)/shard_map/while/body/eval_jaxpr/dot_general | solution.py:65
  247.9 3.0 %copy.18 = f32[128,4096]{1,0:T(8,128)} copy(f32[128,4096]{0,1:T(8,128)} %get-tuple-element.631) | data formatting | bytes 4194304 | tf_op jit(solution)/shard_map/while | solution.py:92
  251.0 3.2 %mul.323 = f32[128,4096]{1,0:T(8,128)} multiply(f32[128,4096]{1,0:T(8,128)S(1)} %copy-done.1, f32[128,4096]{1,0:T(8,128)} %copy.18) | non-fusion elementwise | flops 524288 | bytes 6291456 | tf_op jit(solution)/shard_map/mul | solution.py:168
  (125 shorter events, 42.3 us)
Async XLA Ops:
  7.2 1.2 copy-start
  7.2 3.1 %copy-start.5 = (f32[2048]{0:T(1024)S(1)}, f32[2048]{0:T(1024)}, u32[]{:S(2)}) copy-start(f32[2048]{0:T(1024)} %param.32) | copy-start | bytes 24580
  7.2 3.1 %copy-start.4 = (f32[3,120,128]{2,1,0:T(8,128)S(1)}, f32[3,120,128]{2,1,0:T(8,128)}, u32[]{:S(2)}) copy-start(f32[3,120,128]{2,1,0:T(8,128)} %param.33) | copy-start | bytes 552964
  7.2 65.6 %all-reduce.2.cloned.1.call-start = ((), (), s32[]{:S(2)}) async-start(), calls=%async_computation | async-start | bytes 368640 | tf_op jit(solution)/shard_map/psum | solution.py:139
  10.3 2.2 copy-start.6
  12.6 3.1 %copy-start.7 = (f32[4096]{0:T(1024)S(1)}, f32[4096]{0:T(1024)}, u32[]{:S(2)}) copy-start(f32[4096]{0:T(1024)} %param.21) | copy-start | bytes 49156
  12.6 3.1 %copy-start.8 = (f32[4096]{0:T(1024)S(1)}, f32[4096]{0:T(1024)}, u32[]{:S(2)}) copy-start(f32[4096]{0:T(1024)} %param.22) | copy-start | bytes 49156
  12.6 3.1 %copy-start.2 = (s32[4096]{0:T(1024)S(1)}, s32[4096]{0:T(1024)}, u32[]{:S(2)}) copy-start(s32[4096]{0:T(1024)} %param.25) | copy-start | bytes 49156
  13.4 29.0 %copy-start.9 = (s32[4096]{0:T(1024)S(1)}, s32[4096]{0:T(1024)}, u32[]{:S(2)}) copy-start(s32[4096]{0:T(1024)} %param.24) | copy-start | bytes 49156
  13.4 28.9 %copy-start.11 = (f32[8]{0:T(128)S(1)}, f32[8]{0:T(128)}, u32[]{:S(2)}) copy-start(f32[8]{0:T(128)} %param.28) | copy-start | bytes 100
  13.4 28.9 %copy-start.12 = (f32[8]{0:T(128)S(1)}, f32[8]{0:T(128)}, u32[]{:S(2)}) copy-start(f32[8]{0:T(128)} %param.27) | copy-start | bytes 100
  13.4 28.9 %copy-start.13 = (f32[8]{0:T(128)S(1)}, f32[8]{0:T(128)}, u32[]{:S(2)}) copy-start(f32[8]{0:T(128)} %param.26) | copy-start | bytes 100
  13.4 59.4 %copy-start.10 = (f32[120]{0:T(128)S(1)}, f32[120]{0:T(128)}, u32[]{:S(2)}) copy-start(f32[120]{0:T(128)} %param.29) | copy-start | bytes 1444
  73.7 2.5 copy-start.3
  247.9 3.0 %copy-start.1 = (f32[128,4096]{1,0:T(8,128)S(1)}, f32[128,4096]{1,0:T(8,128)}, u32[]{:S(2)}) copy-start(f32[128,4096]{1,0:T(8,128)} %copy.17) | copy-start | bytes 6291460
Sparse Core Ops, SparseCore 0:
  15.8 56.9 all-reduce.1
